TPU v7x, 32 devices: a whole 2x2x4 slice. The times are simulated.
32 devices in a mesh: egrp: 2 (over x), space: 16 (over z, y, core).
Axes of the slice: x: 2, y: 2, z: 4, core: 2. Of those that a mesh axis runs over, the one named last changes fastest.
Arguments:
- dist: float32 [2, 1024, 64, 128], P(None, 'egrp', 'space'), may hold values from -12 to 12
- hist_x: bfloat16 [4, 2, 1024, 64, 128], P(None, None, 'egrp', 'space'), may hold values from -6 to 6
- hist_g: bfloat16 [4, 2, 1024, 64, 128], P(None, None, 'egrp', 'space'), may hold values from -12 to 12
- mobility: float32 [64, 128], P('space'), may hold values from 0.2 to 2
- region: int32 [64, 128], P('space'), may hold values from 0 to 3
- phonon_bins: int32 [4], replicated, may hold values from 48 to 64, as said below
- coupling: float32 [4], replicated, may hold values from 0.2 to 1.5
- hist_used: int32 [2, 4], replicated, may hold values 0 or 1
Outputs:
- drifted: float32 [2, 1024, 64, 128], P(None, 'egrp', 'space')
Inputs may be any that keep to these rules, and one draw needn't show every extreme that they name: `phonon_bins`: each value lies in 48 to 64; both ends occur.
All inputs are finite; a program needn't handle non-finite values.
Results may differ from a plain program's by a relative error of at most 0.0003.
Values sent between devices are 32-bit elements; how exact they have to be, the bound alone decides.
A program may use at most 128 MiB of HBM per device.

v0:
```python
import jax
import jax.numpy as jnp
from jax import lax
from jax.sharding import PartitionSpec as P

NE = 1024
HISTORY = 4
NREGION = 4
KMAX = 64
COLS = 64


def extended(block, sides, width):
    for axis, dim in sides:
        count = lax.axis_size(axis)
        forward = [(i, i + 1) for i in range(count - 1)]
        backward = [(target, source) for source, target in forward]
        low = lax.ppermute(
            lax.slice_in_dim(block, block.shape[dim] - width, None, axis=dim), axis, forward
        )
        high = lax.ppermute(lax.slice_in_dim(block, 0, width, axis=dim), axis, backward)
        block = jnp.concatenate([low, block, high], axis=dim)
    return block


def add_face(total, field, moved, mobility, moved_mob, valid):
    return total + jnp.where(valid, 0.5 * (mobility + moved_mob) * (moved - field), 0.0)


def local(dist, hist_x, hist_g, mobility, region, phonon_bins, coupling, hist_used):
    width = dist.shape[1]
    rows = dist.shape[2]
    cells = dist.shape[3]
    flat_g = hist_g.reshape(HISTORY, 2, -1)
    energy_ids = lax.axis_index("egrp") * width + jnp.arange(width, dtype=jnp.int32)
    dos = jnp.sqrt((energy_ids.astype(jnp.float32) + 0.5) / NE)
    even = dist[0]
    odd = dist[1]
    outrate = jnp.zeros(even.shape, jnp.float32)
    lam = jnp.zeros(region.shape, jnp.float32)
    for index in range(NREGION):
        offset = phonon_bins[index]
        lower = energy_ids - offset
        upper = energy_ids + offset
        dos_low = jnp.where(
            lower >= 0, jnp.sqrt((jnp.maximum(lower, 0).astype(jnp.float32) + 0.5) / NE), 0.0
        )
        dos_high = jnp.where(upper < NE, jnp.sqrt((upper.astype(jnp.float32) + 0.5) / NE), 0.0)
        rate = coupling[index] * (1.5 * dos_low + 0.5 * dos_high)
        outrate = jnp.where((region == index)[None], rate[:, None, None], outrate)
        lam = jnp.where(region == index, coupling[index], lam)
    column = lax.all_to_all(
        even.reshape(width, rows * cells), "egrp", split_axis=1, concat_axis=0, tiled=True
    )
    span = column.shape[1]
    column_region = lax.dynamic_slice_in_dim(
        region.reshape(-1), lax.axis_index("egrp") * span, span
    )
    padded = jnp.pad(column, ((KMAX, KMAX), (0, 0)))
    total = column.shape[0]
    partial_sum = jnp.zeros(column.shape, jnp.float32)
    for index in range(NREGION):
        offset = phonon_bins[index]
        above = lax.dynamic_slice_in_dim(padded, KMAX + offset, total, 0)
        below = lax.dynamic_slice_in_dim(padded, KMAX - offset, total, 0)
        partial_sum = jnp.where(
            (column_region == index)[None], 1.5 * above + 0.5 * below, partial_sum
        )
    shifted = lax.all_to_all(partial_sum, "egrp", split_axis=0, concat_axis=1, tiled=True).reshape(
        width, rows, cells
    )
    gain_in = lam[None] * dos[:, None, None] * shifted
    new_even = (even + gain_in) / (1.0 + outrate)
    new_odd = odd / (1.0 + outrate + lam[None])
    res = jnp.stack([new_even - even, new_odd - odd])
    res_flat = res.reshape(2, -1)
    cross = jnp.transpose(jnp.sum(flat_g.astype(jnp.float32) * res_flat[None], axis=2))
    self_term = jnp.sum(res_flat * res_flat, axis=1)
    among = lax.dot_general(
        flat_g, flat_g, (((2,), (2,)), ((1,), (1,))), preferred_element_type=jnp.float32
    )
    among, cross, self_term = lax.psum((among, cross, self_term), ("egrp", "space"))
    fields = []
    for field in range(2):
        top = jnp.concatenate([self_term[field][None], cross[field]])[None, :]
        lower_rows = jnp.concatenate([cross[field][:, None], among[field]], axis=1)
        gram = jnp.concatenate([top, lower_rows], axis=0)
        valid = jnp.concatenate([jnp.ones((1,), jnp.float32), hist_used[field].astype(jnp.float32)])
        masked = valid[:, None] * valid[None, :] * gram + jnp.diag(1.0 - valid) * gram[0, 0]
        factor = jnp.linalg.cholesky(masked)
        weights = jax.scipy.linalg.cho_solve((factor, True), valid)
        coeffs = weights / jnp.sum(weights)
        part_mix = coeffs[0] * (dist[field] + 0.5 * res[field])
        for index in range(HISTORY):
            part_mix = part_mix + coeffs[index + 1] * (
                hist_x[index, field].astype(jnp.float32)
                + 0.5 * hist_g[index, field].astype(jnp.float32)
            )
        fields.append(part_mix)
    mixed = jnp.stack(fields)
    mob_block = mobility[None, None]
    wide_field, wide_mob = (
        extended(mixed, (("space", 2),), 1),
        extended(mob_block, (("space", 2),), 1),
    )
    row_ids = lax.axis_index("space") * rows + jnp.arange(rows, dtype=jnp.int32)
    all_rows = lax.axis_size("space") * rows
    cell_ids = jnp.arange(cells, dtype=jnp.int32)
    column_ids = cell_ids % COLS
    lap = jnp.zeros(mixed.shape, jnp.float32)
    lap = add_face(
        lap,
        mixed,
        wide_field[:, :, 0:rows],
        mob_block,
        wide_mob[:, :, 0:rows],
        (row_ids > 0)[:, None],
    )
    lap = add_face(
        lap,
        mixed,
        wide_field[:, :, 2 : rows + 2],
        mob_block,
        wide_mob[:, :, 2 : rows + 2],
        (row_ids < all_rows - 1)[:, None],
    )
    for shift_by, valid_cells in (
        (1, column_ids > 0),
        (-1, column_ids < COLS - 1),
        (COLS, cell_ids >= COLS),
        (-COLS, cell_ids < COLS),
    ):
        moved = jnp.roll(mixed, shift_by, axis=3)
        moved_mob = jnp.roll(mob_block, shift_by, axis=3)
        lap = add_face(lap, mixed, moved, mob_block, moved_mob, valid_cells)
    drive = 0.25 * dos[:, None, None]
    out_even = mixed[0] + 0.08 * lap[0] + drive * mixed[1]
    out_odd = mixed[1] + 0.08 * lap[1] - drive * mixed[0]
    return jnp.stack([out_even, out_odd])


def solution(mesh):
    in_specs = (
        P(None, "egrp", "space", None),
        P(None, None, "egrp", "space", None),
        P(None, None, "egrp", "space", None),
        P("space", None),
        P("space", None),
        P(),
        P(),
        P(),
    )
    out_specs = P(None, "egrp", "space", None)
    return jax.shard_map(local, mesh=mesh, in_specs=in_specs, out_specs=out_specs, check_vma=False)
```

profile of v0, /device:TPU:4, one launch (start us, length us, event | category | flops | bytes accessed | tf_op | source)
XLA Modules:
  0.0 195.0 jit_solution(16239742261708099260)
XLA Ops:
  0.0 1.7 fusion.84
  1.7 1.4 copy.175
  3.1 3.6 %all-to-all-start = ((f32[512,2,256]{0,2,1:T(8,128)}), f32[512,2,256]{0,2,1:T(8,128)S(1)}, u32[]{:S(2)}, u32[]{:S(2)}) async-start(f32[512,2,256]{0,2,1:T(8,128)} %bitcast.6), calls=%async_computation | async-start | bytes 2097152 | tf_op jit(solution)/shard_map/all_to_all | solution.py:52
  6.7 1.9 collective-permute-start
  8.6 3.6 %collective-permute-start.2 = (f32[1,1,1,128]{3,2,1,0:T(1,128)S(1)}, f32[1,1,1,128]{3,2,1,0:T(1,128)S(1)}, u32[]{:S(2)}, u32[]{:S(2)}) collective-permute-start(f32[1,1,1,128]{3,2,1,0:T(1,128)S(1)} %get-tuple-element.54), channel_id=1, source_target_pairs={{1,0},{2,1},{3,2},{4,3},{5,4},{6,5},{7,6},{8,7},{9,8},{10,9},{11,1... | collective-permute-start | bytes 1544 | tf_op jit(solution)/shard_map/ppermute | solution.py:21
  12.3 0.7 fusion.90
  23.1 5.1 %reshape.555 = bf16[4,2,262144]{2,1,0:T(2,128)(2,1)} reshape(bf16[4,2,512,4,128]{4,3,2,1,0:T(4,128)(2,1)} %param.13) | data formatting | bytes 8388608 | tf_op jit(solution)/shard_map/reshape | solution.py:34
  28.2 4.1 %fusion.83 = (bf16[1,1,512,4,128]{4,3,2,1,0:T(4,128)(2,1)}, bf16[1,1,512,4,128]{4,3,2,1,0:T(4,128)(2,1)}, bf16[1,1,512,4,128]{4,3,2,1,0:T(4,128)(2,1)}, bf16[1,1...) fusion(bf16[4,2,512,4,128]{4,3,2,1,0:T(4,128)(2,1)} %param.13), kind=kLoop, calls=%fused_computation.196 | loop fusion | bytes 8388608 | tf_op jit(solution)/shard_map/slice | solution.py:97
  32.5 0.7 fusion.89
  33.2 2.5 %add_multiply_fusion.2 = (f32[512]{0:T(512)S(1)}, f32[512]{0:T(512)S(1)}) fusion(s32[]{:T(128)} %bitcast.10, f32[]{:T(128)} %bitcast.2, s32[]{:T(128)S(6)} %mul.605, s32[]{:T(128)} %bitcast.9, f32[]{:T(128)} %bitcast.1), kind=kLoop, calls=%fused_computation.143 | loop fusion | flops 17920 | bytes 4116 | tf_op jit(solution)/shard_map/mul | solution.py:49
  35.7 2.5 %add_multiply_fusion = (f32[512]{0:T(512)S(1)}, f32[512]{0:T(512)S(1)}) fusion(s32[]{:T(128)} %bitcast.12, f32[]{:T(128)} %bitcast.4, s32[]{:T(128)S(6)} %mul.605, s32[]{:T(128)} %bitcast.11, f32[]{:T(128)} %bitcast.3), kind=kLoop, calls=%fused_computation.141 | loop fusion | flops 17920 | bytes 4116 | tf_op jit(solution)/shard_map/mul | solution.py:49
  38.2 2.4 %select_select_fusion.2 = (f32[4,128]{1,0:T(4,128)S(1)}, pred[4,128]{1,0:T(4,128)(4,1)S(1)}, pred[4,128]{1,0:T(4,128)(4,1)S(1)}, pred[4,128]{1,0:T(4,128)(4,1)S(1)}, pred[4,128]{1,0:T(4,128)(4,1)S(1)}) fusion(f32[]{:T(128)} %bitcast.4, f32[]{:T(128)} %bitcast.3, f32[]{:T(128)} %bitcast.2, f32[]{:T(128)} %bitcast.1, s32[4,128]{1,0:T(4,128)S(1)} %copy-done.22), kind=kLoop, calls=%fused_computation.163 | loop fusion | flops 4096 | bytes 6160 | tf_op jit(solution)/shard_map/jit(_where)/select_n | solution.py:51
  41.0 4.1 %fusion.82 = (bf16[1,1,512,4,128]{4,3,2,1,0:T(4,128)(2,1)}, bf16[1,1,512,4,128]{4,3,2,1,0:T(4,128)(2,1)}, bf16[1,1,512,4,128]{4,3,2,1,0:T(4,128)(2,1)}, bf16[1,1...) fusion(bf16[4,2,512,4,128]{4,3,2,1,0:T(4,128)(2,1)} %param.12), kind=kLoop, calls=%fused_computation.195 | loop fusion | bytes 8388608 | tf_op jit(solution)/shard_map/slice | solution.py:96
  45.1 2.2 %copy.185 = bf16[1,1,512,4,128]{2,4,3,1,0:T(8,128)(2,1)} copy(bf16[1,1,512,4,128]{4,3,2,1,0:T(4,128)(2,1)} %get-tuple-element.22) | data formatting | bytes 1048576
  47.3 1.1 copy.186
  48.4 2.1 %copy.187 = bf16[1,1,512,4,128]{2,4,3,1,0:T(8,128)(2,1)} copy(bf16[1,1,512,4,128]{4,3,2,1,0:T(4,128)(2,1)} %get-tuple-element.21) | data formatting | bytes 1048576
  50.5 1.1 copy.188
  51.7 2.2 %copy.189 = bf16[1,1,512,4,128]{2,4,3,1,0:T(8,128)(2,1)} copy(bf16[1,1,512,4,128]{4,3,2,1,0:T(4,128)(2,1)} %get-tuple-element.20) | data formatting | bytes 1048576
  53.8 2.2 %copy.190 = bf16[1,1,512,4,128]{2,4,3,1,0:T(8,128)(2,1)} copy(bf16[1,1,512,4,128]{4,3,2,1,0:T(4,128)(2,1)} %get-tuple-element.28) | data formatting | bytes 1048576
  56.0 2.1 %copy.191 = bf16[1,1,512,4,128]{2,4,3,1,0:T(8,128)(2,1)} copy(bf16[1,1,512,4,128]{4,3,2,1,0:T(4,128)(2,1)} %get-tuple-element.26) | data formatting | bytes 1048576
  58.1 1.2 copy.192
  59.3 2.2 %copy.177 = bf16[1,1,512,4,128]{2,4,3,1,0:T(8,128)(2,1)} copy(bf16[1,1,512,4,128]{4,3,2,1,0:T(4,128)(2,1)} %get-tuple-element.19) | data formatting | bytes 1048576
  61.5 1.2 copy.178
  62.7 1.1 copy.179
  64.5 2.3 %fusion.25 = f32[1024,256]{1,0:T(8,128)} fusion(s32[]{:T(128)S(6)} %select_n.228, f32[1024,256]{1,0:T(8,128)S(1)} %bitcast.141, s32[]{:T(128)S(6)} %select_n.229, s32[]{:T(128)S(6)} %select_n.230, s32[]{:T(128)S(6)} %select_n.231, s32[]{:T(128)S(6)} %select_n.232, s32[]{:T(128)S(6)} %select_n.233, s32[]{:T(128)S(6)} %select_n.234, s32[]{:T(128)S(6)} %select_n.235, ...), kind=kLoop, calls=%fused_computation.64 | loop fusion | flops 4194304 | bytes 2098208 | tf_op jit(solution)/shard_map/jit(_where)/select_n | solution.py:66
  66.7 3.8 %all-to-all-start.1 = ((f32[2,512,256]{2,1,0:T(8,128)}), f32[2,512,256]{2,1,0:T(8,128)S(1)}, u32[]{:S(2)}, u32[]{:S(2)}) async-start(f32[2,512,256]{2,1,0:T(8,128)} %bitcast.13), calls=%async_computation.1 | async-start | bytes 2097152 | tf_op jit(solution)/shard_map/all_to_all | solution.py:69
  70.5 9.5 %fusion = f32[2,4,4]{2,1,0:T(4,128)S(1)} fusion(bf16[4,2,262144]{2,1,0:T(2,128)(2,1)} %reshape.555), kind=kOutput, calls=%fused_computation.18 | convolution fusion | flops 16777216 | bytes 4194432 | tf_op jit(solution)/shard_map/dot_general | solution.py:79
  80.0 2.2 %copy.180 = bf16[1,1,512,4,128]{2,4,3,1,0:T(8,128)(2,1)} copy(bf16[1,1,512,4,128]{4,3,2,1,0:T(4,128)(2,1)} %get-tuple-element.33) | data formatting | bytes 1048576
  82.3 2.1 %copy.181 = bf16[1,1,512,4,128]{2,4,3,1,0:T(8,128)(2,1)} copy(bf16[1,1,512,4,128]{4,3,2,1,0:T(4,128)(2,1)} %get-tuple-element.24) | data formatting | bytes 1048576
  84.4 1.1 copy.182
  85.5 2.1 %copy.183 = bf16[1,1,512,4,128]{2,4,3,1,0:T(8,128)(2,1)} copy(bf16[1,1,512,4,128]{4,3,2,1,0:T(4,128)(2,1)} %get-tuple-element.23) | data formatting | bytes 1048576
  87.6 1.1 copy.184
  88.7 1.3 copy.141
  90.0 2.3 %divide_subtract_fusion.1 = (f32[1,512,4,128]{1,3,2,0:T(8,128)S(1)}, f32[1,512,4,128]{1,3,2,0:T(8,128)S(1)}) fusion(f32[1,512,4,128]{1,3,2,0:T(8,128)} %copy.175, f32[1,512,4,128]{1,3,2,0:T(8,128)} %bitcast.146, f32[512]{0:T(512)S(1)} %get-tuple-element.98, f32[512]{0:T(512)S(1)} %get-tuple-element.99, f32[512]{0:T(512)S(1)} %get-tuple-element.100, ...), kind=kLoop, calls=%fused_computation.94 | loop fusion | flops 3407872 | bytes 5257216 | tf_op jit(solution)/shard_map/sub | solution.py:75
  92.4 1.3 copy.142
  93.7 1.3 copy.144
  95.0 1.6 pad_maximum_fusion.5
  96.6 2.9 %copy.145 = f32[2,512,4,128]{3,2,1,0:T(4,128)} copy(f32[2,512,4,128]{1,3,2,0:T(8,128)} %pad_maximum_fusion.5) | data formatting | bytes 4194304 | tf_op jit(solution)/shard_map/stack | solution.py:75
  99.5 5.3 %multiply_reduce_fusion = f32[4,2]{1,0:T(4,128)S(1)} fusion(bf16[4,2,512,4,128]{4,3,2,1,0:T(4,128)(2,1)} %param.13, f32[2,512,4,128]{3,2,1,0:T(4,128)} %copy.145), kind=kLoop, calls=%fused_computation | loop fusion | flops 6291448 | bytes 6291488 | tf_op jit(solution)/shard_map/reduce_sum | solution.py:77
  104.9 2.3 %fusion.15 = f32[2]{0:T(128)S(1)} fusion(f32[1,262144]{1,0:T(1,128)S(1)} %bitcast.143, f32[1,262144]{1,0:T(1,128)S(1)} %bitcast.142), kind=kLoop, calls=%fused_computation.38 | loop fusion | flops 1572862 | bytes 2097160 | tf_op jit(solution)/shard_map/reduce_sum | solution.py:78
  107.2 42.1 %all-reduce.1 = (f32[2,4,4]{2,1,0:T(4,128)S(1)}, f32[2,4]{0,1:T(4,128)S(1)}, f32[2]{0:T(128)S(1)}) all-reduce(f32[2,4,4]{2,1,0:T(4,128)S(1)} %fusion, f32[2,4]{0,1:T(4,128)S(1)} %bitcast.152, f32[2]{0:T(128)S(1)} %fusion.15), channel_id=1, replica_groups=mesh['egrp'=2,'space'=16] {'egrp','space'}, use_global_device_ids=true, to_apply=%region_4.5 | all-reduce | flops 42 | bytes 336 | tf_op jit(solution)/shard_map/psum | solution.py:82
  149.3 0.6 fusion.87
  150.1 0.7 maximum_bitcast_fusion.1
  151.3 0.4 cholesky.55
  151.8 0.7 compare_reduce_fusion
  152.5 0.6 fusion.50
  153.7 0.8 fusion.92
  154.5 0.6 broadcast_divide_fusion
  155.1 0.6 fusion.88
  155.7 0.7 maximum_bitcast_fusion
  157.4 0.6 compare_reduce_fusion.1
  158.1 0.6 fusion.49
  159.3 0.8 fusion.91
  160.1 0.6 broadcast_divide_fusion.1
  160.7 0.7 fusion.86
  161.5 6.4 %bitcast_add_fusion = f32[1,512,4,128]{1,3,2,0:T(8,128)S(1)} fusion(bf16[1,1,512,4,128]{2,4,3,1,0:T(8,128)(2,1)} %copy.192, bf16[1,1,512,4,128]{2,4,3,1,0:T(8,128)(2,1)} %copy.191, bf16[1,1,512,4,128]{2,4,3,1,0:T(8,128)(2,1)} %copy.190, bf16[1,1,512,4,128]{2,4,3,1,0:T(8,128)(2,1)} %copy.189, bf16[1,1,512,4,128]{2,4,3,1,0:T(8,128)(2,1)} %copy.188, ...), kind=kLoop, calls=%fused_computation.86 | loop fusion | flops 9175040 | bytes 6303764 | tf_op jit(solution)/shard_map/add | solution.py:95
  167.9 5.4 %bitcast_add_fusion.4 = f32[1,512,4,128]{1,3,2,0:T(8,128)S(1)} fusion(bf16[1,1,512,4,128]{2,4,3,1,0:T(8,128)(2,1)S(1)} %copy-done.18, bf16[1,1,512,4,128]{2,4,3,1,0:T(8,128)(2,1)S(1)} %copy-done.17, bf16[1,1,512,4,128]{2,4,3,1,0:T(8,128)(2,1)S(1)} %copy-done.16, bf16[1,1,512,4,128]{2,4,3,1,0:T(8,128)(2,1)S(1)} %copy-done.15, ...), kind=kLoop, calls=%fused_computation.90 | loop fusion | flops 7077888 | bytes 7340052 | tf_op jit(solution)/shard_map/add | solution.py:95
  173.3 1.9 collective-permute-start.1
  175.3 3.6 %collective-permute-start.3 = (f32[2,512,1,128]{1,3,2,0:T(8,128)S(1)}, f32[2,512,1,128]{1,3,2,0:T(8,128)S(1)}, u32[]{:S(2)}, u32[]{:S(2)}) collective-permute-start(f32[2,512,1,128]{1,3,2,0:T(8,128)S(1)} %get-tuple-element.42), channel_id=1, source_target_pairs={{1,0},{2,1},{3,2},{4,3},{5,4},{6,5},{7,6},{8,7},{9,8},{10,9},{11,1... | collective-permute-start | bytes 1572872 | tf_op jit(solution)/shard_map/ppermute | solution.py:21
  179.2 0.5 fusion.3
  179.7 9.7 %collective-permute-done.1 = f32[2,512,1,128]{1,3,2,0:T(8,128)S(1)} collective-permute-done((f32[2,512,1,128]{1,3,2,0:T(8,128)S(1)}, f32[2,512,1,128]{1,3,2,0:T(8,128)S(1)}, u32[]{:S(2)}, u32[]{:S(2)}) %collective-permute-start.1) | collective-permute-done | bytes 524320 | tf_op jit(solution)/shard_map/ppermute | solution.py:18
  189.5 2.9 %fusion.11 = f32[2,512,4,128]{1,3,2,0:T(8,128)S(1)} fusion(f32[2,512,1,128]{1,3,2,0:T(8,128)S(1)} %collective-permute-done.3, f32[1,512,4,128]{1,3,2,0:T(8,128)S(1)} %bitcast_add_fusion, f32[1,512,4,128]{1,3,2,0:T(8,128)S(1)} %bitcast_add_fusion.4, f32[2,512,1,128]{1,3,2,0:T(8,128)S(1)} %collective-permute-done.1, ...), kind=kLoop, calls=%fused_computation.30 | loop fusion | flops 15204352 | bytes 11545096 | tf_op jit(solution)/shard_map/add | solution.py:27
  192.4 0.5 fusion.44
  193.2 1.8 copy.174
  (93 shorter events, 4.8 us)
Async XLA Ops:
  1.7 5.0 %copy-start.19 = (f32[4,128]{1,0:T(4,128)S(1)}, f32[4,128]{1,0:T(4,128)}, u32[]{:S(2)}) copy-start(f32[4,128]{1,0:T(4,128)} %param.14) | copy-start | bytes 6148
  1.7 10.6 %copy-start.20 = (s32[4]{0:T(128)S(1)}, s32[4]{0:T(128)}, u32[]{:S(2)}) copy-start(s32[4]{0:T(128)} %param.16) | copy-start | bytes 52
  3.1 61.0 %all-to-all-start = ((f32[512,2,256]{0,2,1:T(8,128)}), f32[512,2,256]{0,2,1:T(8,128)S(1)}, u32[]{:S(2)}, u32[]{:S(2)}) async-start(f32[512,2,256]{0,2,1:T(8,128)} %bitcast.6), calls=%async_computation | async-start | bytes 2097152 | tf_op jit(solution)/shard_map/all_to_all | solution.py:52
  6.7 82.0 %collective-permute-start = (f32[1,1,1,128]{3,2,1,0:T(1,128)S(1)}, f32[1,1,1,128]{3,2,1,0:T(1,128)S(1)}, u32[]{:S(2)}, u32[]{:S(2)}) collective-permute-start(f32[1,1,1,128]{3,2,1,0:T(1,128)S(1)} %get-tuple-element.53), channel_id=1, source_target_pairs={{0,1},{1,2},{2,3},{3,4},{4,5},{5,6},{6,7},{7,8},{8,9},{9,10},{10,1... | collective-permute-start | bytes 1544 | tf_op jit(solution)/shard_map/ppermute | solution.py:18
  8.6 80.1 %collective-permute-start.2 = (f32[1,1,1,128]{3,2,1,0:T(1,128)S(1)}, f32[1,1,1,128]{3,2,1,0:T(1,128)S(1)}, u32[]{:S(2)}, u32[]{:S(2)}) collective-permute-start(f32[1,1,1,128]{3,2,1,0:T(1,128)S(1)} %get-tuple-element.54), channel_id=1, source_target_pairs={{1,0},{2,1},{3,2},{4,3},{5,4},{6,5},{7,6},{8,7},{9,8},{10,9},{11,1... | collective-permute-start | bytes 1544 | tf_op jit(solution)/shard_map/ppermute | solution.py:21
  28.2 4.3 %copy-start.21 = (f32[4]{0:T(128)S(1)}, f32[4]{0:T(128)}, u32[]{:S(2)}) copy-start(f32[4]{0:T(128)} %param.17) | copy-start | bytes 52
  28.2 10.0 %copy-start.22 = (s32[4,128]{1,0:T(4,128)S(1)}, s32[4,128]{1,0:T(4,128)}, u32[]{:S(2)}) copy-start(s32[4,128]{1,0:T(4,128)} %param.15) | copy-start | bytes 6148
  32.3 8.7 %copy-start.23 = (s32[2,4]{1,0:T(2,128)S(1)}, s32[2,4]{1,0:T(2,128)}, u32[]{:S(2)}) copy-start(s32[2,4]{1,0:T(2,128)} %param.18) | copy-start | bytes 100
  41.0 6.3 %copy-start.7 = (bf16[1,1,512,4,128]{4,3,2,1,0:T(4,128)(2,1)S(1)}, bf16[1,1,512,4,128]{4,3,2,1,0:T(4,128)(2,1)}, u32[]{:S(2)}) copy-start(bf16[1,1,512,4,128]{4,3,2,1,0:T(4,128)(2,1)} %get-tuple-element.30) | copy-start | bytes 1572868
  45.1 5.4 %copy-start.6 = (bf16[1,1,512,4,128]{4,3,2,1,0:T(4,128)(2,1)S(1)}, bf16[1,1,512,4,128]{4,3,2,1,0:T(4,128)(2,1)}, u32[]{:S(2)}) copy-start(bf16[1,1,512,4,128]{4,3,2,1,0:T(4,128)(2,1)} %get-tuple-element.29) | copy-start | bytes 1572868
  50.5 7.6 %copy-start.5 = (bf16[1,1,512,4,128]{4,3,2,1,0:T(4,128)(2,1)S(1)}, bf16[1,1,512,4,128]{4,3,2,1,0:T(4,128)(2,1)}, u32[]{:S(2)}) copy-start(bf16[1,1,512,4,128]{4,3,2,1,0:T(4,128)(2,1)} %get-tuple-element.34) | copy-start | bytes 1572868
  53.8 7.7 %copy-start.4 = (bf16[1,1,512,4,128]{4,3,2,1,0:T(4,128)(2,1)S(1)}, bf16[1,1,512,4,128]{4,3,2,1,0:T(4,128)(2,1)}, u32[]{:S(2)}) copy-start(bf16[1,1,512,4,128]{4,3,2,1,0:T(4,128)(2,1)} %get-tuple-element.27) | copy-start | bytes 1572868
  59.3 3.4 %copy-start.8 = (bf16[1,1,512,4,128]{4,3,2,1,0:T(4,128)(2,1)S(1)}, bf16[1,1,512,4,128]{4,3,2,1,0:T(4,128)(2,1)}, u32[]{:S(2)}) copy-start(bf16[1,1,512,4,128]{4,3,2,1,0:T(4,128)(2,1)} %get-tuple-element.25) | copy-start | bytes 1572868
  66.7 22.0 %all-to-all-start.1 = ((f32[2,512,256]{2,1,0:T(8,128)}), f32[2,512,256]{2,1,0:T(8,128)S(1)}, u32[]{:S(2)}, u32[]{:S(2)}) async-start(f32[2,512,256]{2,1,0:T(8,128)} %bitcast.13), calls=%async_computation.1 | async-start | bytes 2097152 | tf_op jit(solution)/shard_map/all_to_all | solution.py:69
  80.0 4.3 %copy-start.3 = (bf16[1,1,512,4,128]{4,3,2,1,0:T(4,128)(2,1)S(1)}, bf16[1,1,512,4,128]{4,3,2,1,0:T(4,128)(2,1)}, u32[]{:S(2)}) copy-start(bf16[1,1,512,4,128]{4,3,2,1,0:T(4,128)(2,1)} %get-tuple-element.32) | copy-start | bytes 1572868
  80.0 7.5 %copy-start.2 = (bf16[1,1,512,4,128]{4,3,2,1,0:T(4,128)(2,1)S(1)}, bf16[1,1,512,4,128]{4,3,2,1,0:T(4,128)(2,1)}, u32[]{:S(2)}) copy-start(bf16[1,1,512,4,128]{4,3,2,1,0:T(4,128)(2,1)} %get-tuple-element.31) | copy-start | bytes 1572868
  99.5 5.3 %copy-start = (f32[1,512,4,128]{3,2,1,0:T(4,128)S(1)}, f32[1,512,4,128]{3,2,1,0:T(4,128)}, u32[]{:S(2)}) copy-start(f32[1,512,4,128]{3,2,1,0:T(4,128)} %copy.142) | copy-start | bytes 3145732
  99.5 5.3 %copy-start.1 = (f32[1,512,4,128]{3,2,1,0:T(4,128)S(1)}, f32[1,512,4,128]{3,2,1,0:T(4,128)}, u32[]{:S(2)}) copy-start(f32[1,512,4,128]{3,2,1,0:T(4,128)} %copy.144) | copy-start | bytes 3145732
  104.9 56.5 %copy-start.9 = (bf16[1,1,512,4,128]{2,4,3,1,0:T(8,128)(2,1)S(1)}, bf16[1,1,512,4,128]{2,4,3,1,0:T(8,128)(2,1)}, u32[]{:S(2)}) copy-start(bf16[1,1,512,4,128]{2,4,3,1,0:T(8,128)(2,1)} %copy.185) | copy-start | bytes 1572868
  104.9 56.5 %copy-start.11 = (bf16[1,1,512,4,128]{2,4,3,1,0:T(8,128)(2,1)S(1)}, bf16[1,1,512,4,128]{2,4,3,1,0:T(8,128)(2,1)}, u32[]{:S(2)}) copy-start(bf16[1,1,512,4,128]{2,4,3,1,0:T(8,128)(2,1)} %copy.186) | copy-start | bytes 1572868
  161.4 6.4 %copy-start.10 = (bf16[1,1,512,4,128]{2,4,3,1,0:T(8,128)(2,1)S(1)}, bf16[1,1,512,4,128]{2,4,3,1,0:T(8,128)(2,1)}, u32[]{:S(2)}) copy-start(bf16[1,1,512,4,128]{2,4,3,1,0:T(8,128)(2,1)} %copy.177) | copy-start | bytes 1572868
  161.4 6.4 %copy-start.12 = (bf16[1,1,512,4,128]{2,4,3,1,0:T(8,128)(2,1)S(1)}, bf16[1,1,512,4,128]{2,4,3,1,0:T(8,128)(2,1)}, u32[]{:S(2)}) copy-start(bf16[1,1,512,4,128]{2,4,3,1,0:T(8,128)(2,1)} %copy.178) | copy-start | bytes 1572868
  161.4 6.4 %copy-start.13 = (bf16[1,1,512,4,128]{2,4,3,1,0:T(8,128)(2,1)S(1)}, bf16[1,1,512,4,128]{2,4,3,1,0:T(8,128)(2,1)}, u32[]{:S(2)}) copy-start(bf16[1,1,512,4,128]{2,4,3,1,0:T(8,128)(2,1)} %copy.179) | copy-start | bytes 1572868
  161.4 6.4 %copy-start.14 = (bf16[1,1,512,4,128]{2,4,3,1,0:T(8,128)(2,1)S(1)}, bf16[1,1,512,4,128]{2,4,3,1,0:T(8,128)(2,1)}, u32[]{:S(2)}) copy-start(bf16[1,1,512,4,128]{2,4,3,1,0:T(8,128)(2,1)} %copy.180) | copy-start | bytes 1572868
  161.4 6.4 %copy-start.15 = (bf16[1,1,512,4,128]{2,4,3,1,0:T(8,128)(2,1)S(1)}, bf16[1,1,512,4,128]{2,4,3,1,0:T(8,128)(2,1)}, u32[]{:S(2)}) copy-start(bf16[1,1,512,4,128]{2,4,3,1,0:T(8,128)(2,1)} %copy.181) | copy-start | bytes 1572868
  161.4 6.4 %copy-start.16 = (bf16[1,1,512,4,128]{2,4,3,1,0:T(8,128)(2,1)S(1)}, bf16[1,1,512,4,128]{2,4,3,1,0:T(8,128)(2,1)}, u32[]{:S(2)}) copy-start(bf16[1,1,512,4,128]{2,4,3,1,0:T(8,128)(2,1)} %copy.182) | copy-start | bytes 1572868
  161.5 6.4 %copy-start.17 = (bf16[1,1,512,4,128]{2,4,3,1,0:T(8,128)(2,1)S(1)}, bf16[1,1,512,4,128]{2,4,3,1,0:T(8,128)(2,1)}, u32[]{:S(2)}) copy-start(bf16[1,1,512,4,128]{2,4,3,1,0:T(8,128)(2,1)} %copy.183) | copy-start | bytes 1572868
  161.5 6.4 %copy-start.18 = (bf16[1,1,512,4,128]{2,4,3,1,0:T(8,128)(2,1)S(1)}, bf16[1,1,512,4,128]{2,4,3,1,0:T(8,128)(2,1)}, u32[]{:S(2)}) copy-start(bf16[1,1,512,4,128]{2,4,3,1,0:T(8,128)(2,1)} %copy.184) | copy-start | bytes 1572868
  173.3 16.1 %collective-permute-start.1 = (f32[2,512,1,128]{1,3,2,0:T(8,128)S(1)}, f32[2,512,1,128]{1,3,2,0:T(8,128)S(1)}, u32[]{:S(2)}, u32[]{:S(2)}) collective-permute-start(f32[2,512,1,128]{1,3,2,0:T(8,128)S(1)} %get-tuple-element.41), channel_id=1, source_target_pairs={{0,1},{1,2},{2,3},{3,4},{4,5},{5,6},{6,7},{7,8},{8,9},{9,10},{10,1... | collective-permute-start | bytes 1572872 | tf_op jit(solution)/shard_map/ppermute | solution.py:18
  175.3 14.2 %collective-permute-start.3 = (f32[2,512,1,128]{1,3,2,0:T(8,128)S(1)}, f32[2,512,1,128]{1,3,2,0:T(8,128)S(1)}, u32[]{:S(2)}, u32[]{:S(2)}) collective-permute-start(f32[2,512,1,128]{1,3,2,0:T(8,128)S(1)} %get-tuple-element.42), channel_id=1, source_target_pairs={{1,0},{2,1},{3,2},{4,3},{5,4},{6,5},{7,6},{8,7},{9,8},{10,9},{11,1... | collective-permute-start | bytes 1572872 | tf_op jit(solution)/shard_map/ppermute | solution.py:21
where the time goes:
time: 197 us; the launch traced here: 195 us
  local copies, waits for them, and re-layouts  57.4 us (29%)
  other arithmetic  45.2 us (23%)
  blocking collectives  42.1 us (21%)
  starting transfers between devices  18.5 us (9%)
  matrix products  11.5 us (6%)
  between operations  10.7 us (5%)
  waiting for transfers between devices  9.76 us (5%)
    psum x1, blocking collectives, local(): lax.psum((among, cross, self_term), ('egrp', 'space'))  42.1 us
    unnamed x66, local copies, waits for them, and re-layouts  29.2 us
    add x2, other arithmetic, local(): part_mix + coeffs[index + 1] * (hist_x[index, field].astype(jnp.float32)...  11.7 us
    ppermute x2, waiting for transfers between devices, extended(): lax.ppermute(lax.slice_in_dim(block, block.shape[dim] - width, None, axis...  9.75 us
    dot_general x1, matrix products, local(): lax.dot_general(flat_g, flat_g, (((2,), (2,)), ((1,), (1,))), preferred_e...  9.54 us
    ppermute x2, starting transfers between devices, extended(): lax.ppermute(lax.slice_in_dim(block, 0, width, axis=dim), axis, backward)  7.28 us
    reduce_sum x1, other arithmetic, local(): jnp.sum(flat_g.astype(jnp.float32) * res_flat[None], axis=2)  5.32 us
    reshape x1, local copies, waits for them, and re-layouts, local(): flat_g = hist_g.reshape(HISTORY, 2, -1)  5.11 us
  transfers between devices with their start and end apart: 6, of which 1 were waited for; matrix products, arithmetic and copies ran while one was open for 32% of the time, Pallas kernels for 0%

commit v1 on v0

v1 whole, which is shorter than its diff:
```python
import functools
import jax
import jax.numpy as jnp
from jax import lax
from jax.experimental import pallas as pl
from jax.experimental.pallas import tpu as pltpu
from jax.sharding import PartitionSpec as P

NE = 1024
HISTORY = 4
NREGION = 4
KMAX = 64
COLS = 64
PIECES = 4
STEP = 16
PAIRS = [(i, j) for i in range(HISTORY + 1) for j in range(i, HISTORY + 1)]
MESH = pl.DeviceIdType.MESH


def dos_of(energy):
    return jnp.sqrt((energy.astype(jnp.float32) + 0.5) * (1.0 / NE))


def solve(total, field, used_ref):
    def entry(i, j):
        lane = field * len(PAIRS) + PAIRS.index((min(i, j), max(i, j)))
        return jnp.broadcast_to(total[:, lane : lane + 1], (8, 128))

    size = HISTORY + 1
    valid = [jnp.ones((8, 128), jnp.float32)]
    for index in range(HISTORY):
        valid.append(jnp.full((8, 128), used_ref[field, index].astype(jnp.float32)))
    first = entry(0, 0)
    low = [[None] * size for _ in range(size)]
    scaled = [[None] * size for _ in range(size)]
    inverse = [None] * size
    for j in range(size):
        for i in range(j, size):
            value = valid[i] * valid[j] * entry(i, j)
            if i == j:
                value = value + (1.0 - valid[i]) * first
            for k in range(j):
                value = value - scaled[i][k] * low[j][k]
            scaled[i][j] = value
        inverse[j] = 1.0 / scaled[j][j]
        for i in range(j + 1, size):
            low[i][j] = scaled[i][j] * inverse[j]
    forward = []
    for i in range(size):
        value = valid[i]
        for k in range(i):
            value = value - low[i][k] * forward[k]
        forward.append(value)
    weights = [None] * size
    for i in reversed(range(size)):
        value = forward[i] * inverse[i]
        for k in range(i + 1, size):
            value = value - low[k][i] * weights[k]
        weights[i] = value
    inv_sum = 1.0 / functools.reduce(lambda a, b: a + b, weights)
    return [w * inv_sum for w in weights]


def kernel(
    n_egrp, n_space, ne, rows,
    bins_ref, coup_ref, used_ref, mob_ref, region_ref, dist_hbm, hx_hbm, hg_hbm,
    out_hbm,
    even, odd, hg, hx, base, hist, mixed, out, lo, hi, offs, lam_ref, tile, weight,
    mob_send, mob_lo, mob_hi, sums, part, gathered, halo,
    in_sem, out_sem, halo_send, halo_recv, mob_ssem, mob_rsem, sum_send, sum_recv,
    edge_send, edge_recv,
):
    my_e = lax.axis_index("egrp")
    my_s = lax.axis_index("space")
    count = n_egrp * n_space
    me = my_e * n_space + my_s
    total_rows = ne * rows
    pad = KMAX * rows

    def device(index):
        return (index // n_space, lax.rem(index, n_space))

    loads = [
        pltpu.make_async_copy(dist_hbm.at[0], even.at[pl.ds(pad, total_rows)], in_sem.at[0]),
        pltpu.make_async_copy(dist_hbm.at[1], odd, in_sem.at[1]),
    ]
    for index in range(HISTORY):
        loads.append(pltpu.make_async_copy(hg_hbm.at[index], hg.at[index], in_sem.at[2 + index]))
    late = [
        pltpu.make_async_copy(hx_hbm.at[index], hx.at[index], in_sem.at[2 + HISTORY + index])
        for index in range(HISTORY)
    ]
    for copy in loads + late:
        copy.start()

    barrier = pltpu.get_barrier_semaphore()

    def greet(step, carry):
        pl.semaphore_signal(
            barrier, inc=1, device_id=device(lax.rem(me + step, count)), device_id_type=MESH
        )
        return carry

    lax.fori_loop(1, count, greet, 0)

    for copy_of in range(STEP // rows):
        tile[pl.ds(copy_of * rows, rows), :] = region_ref[...]
    region = tile[...]
    inside = [region == index for index in range(NREGION)]
    bins = jnp.zeros((STEP, 128), jnp.int32)
    lam = jnp.zeros((STEP, 128), jnp.float32)
    for index in range(NREGION):
        bins = jnp.where(inside[index], bins_ref[index], bins)
        lam = jnp.where(inside[index], coup_ref[index], lam)
    offs[...] = bins
    lam_ref[...] = lam
    mob_send[0] = mob_ref[0:1, :]
    mob_send[1] = mob_ref[rows - 1 : rows, :]

    has_below_e = my_e > 0
    has_above_e = my_e < n_egrp - 1
    has_below = my_s > 0
    has_above = my_s < n_space - 1

    even[pl.ds(0, pad), :] = jnp.zeros((pad, 128), jnp.float32)
    even[pl.ds(pad + total_rows, pad), :] = jnp.zeros((pad, 128), jnp.float32)

    @pl.when(my_s == 0)
    def _():
        lo[...] = jnp.zeros(lo.shape, jnp.float32)
        mob_lo[...] = jnp.zeros(mob_lo.shape, jnp.float32)

    @pl.when(my_s == n_space - 1)
    def _():
        hi[...] = jnp.zeros(hi.shape, jnp.float32)
        mob_hi[...] = jnp.zeros(mob_hi.shape, jnp.float32)

    pl.semaphore_wait(barrier, count - 1)

    up_e = pltpu.make_async_remote_copy(
        dist_hbm.at[0, pl.ds(total_rows - pad, pad)], halo.at[0],
        halo_send.at[0], halo_recv.at[0],
        device_id=(lax.rem(my_e + 1, n_egrp), my_s), device_id_type=MESH,
    )
    down_e = pltpu.make_async_remote_copy(
        dist_hbm.at[0, pl.ds(0, pad)], halo.at[1],
        halo_send.at[1], halo_recv.at[1],
        device_id=(lax.rem(my_e + n_egrp - 1, n_egrp), my_s), device_id_type=MESH,
    )
    next_s = lax.rem(my_s + 1, n_space)
    prev_s = lax.rem(my_s + n_space - 1, n_space)
    up_mob = pltpu.make_async_remote_copy(
        mob_send.at[1], mob_lo, mob_ssem.at[0], mob_rsem.at[0],
        device_id=(my_e, next_s), device_id_type=MESH,
    )
    down_mob = pltpu.make_async_remote_copy(
        mob_send.at[0], mob_hi, mob_ssem.at[1], mob_rsem.at[1],
        device_id=(my_e, prev_s), device_id_type=MESH,
    )

    @pl.when(has_above_e)
    def _():
        up_e.start()

    @pl.when(has_below_e)
    def _():
        down_e.start()

    @pl.when(has_above)
    def _():
        up_mob.start()

    @pl.when(has_below)
    def _():
        down_mob.start()

    for copy in loads:
        copy.wait()

    def residuals(step, accs):
        row = pl.multiple_of(step * STEP, STEP)
        bins = offs[...]
        lam = lam_ref[...]
        energy = my_e * ne + (row + lax.broadcasted_iota(jnp.int32, (STEP, 128), 0)) // rows
        region = tile[...]
        above = None
        for index in range(NREGION):
            shift = bins_ref[index] * rows
            up = even[pl.ds(pad + row + shift, STEP), :]
            down = even[pl.ds(pad + row - shift, STEP), :]
            if above is None:
                above, below = up, down
            else:
                above = jnp.where(region == index, up, above)
                below = jnp.where(region == index, down, below)
        lower = energy - bins
        upper = energy + bins
        dos_low = jnp.where(lower >= 0, dos_of(jnp.maximum(lower, 0)), 0.0)
        dos_high = jnp.where(upper < NE, dos_of(upper), 0.0)
        loss = 1.0 + lam * (1.5 * dos_low + 0.5 * dos_high)
        own_even = even[pl.ds(pad + row, STEP), :]
        own_odd = odd[pl.ds(row, STEP), :]
        gain = lam * dos_of(energy) * (1.5 * above + 0.5 * below)
        res = [
            (own_even + gain) * (1.0 / loss) - own_even,
            own_odd * (1.0 / (loss + lam)) - own_odd,
        ]
        base[0, pl.ds(row, STEP), :] = own_even + 0.5 * res[0]
        base[1, pl.ds(row, STEP), :] = own_odd + 0.5 * res[1]
        new = []
        for field in range(2):
            vectors = [res[field]] + [
                hg[index, field, pl.ds(row, STEP), :].astype(jnp.float32)
                for index in range(HISTORY)
            ]
            for position, (i, j) in enumerate(PAIRS):
                product = vectors[i] * vectors[j]
                new.append(accs[field * len(PAIRS) + position] + (product[:8] + product[8:]))
        return tuple(new)

    accs = tuple(jnp.zeros((8, 128), jnp.float32) for _ in range(2 * len(PAIRS)))
    edge = pad // STEP
    steps = total_rows // STEP
    accs = lax.fori_loop(edge, steps - edge, residuals, accs)

    @pl.when(has_below_e)
    def _():
        up_e.wait_recv()
        even[pl.ds(0, pad), :] = halo[0]

    accs = lax.fori_loop(0, edge, residuals, accs)

    @pl.when(has_above_e)
    def _():
        down_e.wait_recv()
        even[pl.ds(pad + total_rows, pad), :] = halo[1]

    accs = lax.fori_loop(steps - edge, steps, residuals, accs)

    sums[...] = jnp.zeros(sums.shape, jnp.float32)
    for position, acc in enumerate(accs):
        sums[position : position + 1, :] = jnp.sum(acc, axis=0, keepdims=True)
    lane_sum = jnp.sum(sums[...], axis=1, keepdims=True)
    place = lax.broadcasted_iota(jnp.int32, sums.shape, 0) == lax.broadcasted_iota(
        jnp.int32, sums.shape, 1
    )
    row_sum = jnp.sum(jnp.where(place, lane_sum, 0.0), axis=0, keepdims=True)
    part[...] = row_sum
    gathered[me] = row_sum

    def send_sums(step, carry):
        pltpu.make_async_remote_copy(
            part, gathered.at[me], sum_send, sum_recv,
            device_id=device(lax.rem(me + step, count)), device_id_type=MESH,
        ).start()
        return carry

    lax.fori_loop(1, count, send_sums, 0)

    for copy in late:
        copy.wait()

    def join_history(step, carry):
        row = pl.multiple_of(step * STEP, STEP)
        for index in range(HISTORY):
            for field in range(2):
                hist[index, field, pl.ds(row, STEP), :] = hx[
                    index, field, pl.ds(row, STEP), :
                ].astype(jnp.float32) + 0.5 * hg[index, field, pl.ds(row, STEP), :].astype(
                    jnp.float32
                )
        return carry

    lax.fori_loop(0, steps, join_history, 0)

    @pl.when(has_below)
    def _():
        up_mob.wait_recv()

    @pl.when(has_above)
    def _():
        down_mob.wait_recv()

    lanes = lax.broadcasted_iota(jnp.int32, (1, 128), 1)
    column = lanes % COLS
    for row in range(rows):
        mob = mob_ref[row : row + 1, :]
        under = mob_lo[...] if row == 0 else mob_ref[row - 1 : row, :]
        over = mob_hi[...] if row == rows - 1 else mob_ref[row + 1 : row + 2, :]
        w_under = 0.04 * (mob + under)
        w_over = 0.04 * (mob + over)
        if row == 0:
            w_under = jnp.where(has_below, w_under, 0.0)
        if row == rows - 1:
            w_over = jnp.where(has_above, w_over, 0.0)
        w_left = jnp.where(column > 0, 0.04 * (mob + pltpu.roll(mob, 1, 1)), 0.0)
        w_right = jnp.where(column < COLS - 1, 0.04 * (mob + pltpu.roll(mob, 127, 1)), 0.0)
        w_plane = 0.04 * (mob + pltpu.roll(mob, COLS, 1))
        own = 1.0 - (w_under + w_over + w_left + w_right + w_plane)
        for place, value in enumerate((own, w_under, w_over, w_left, w_right, w_plane)):
            weight[row, place] = jnp.broadcast_to(value, (8, 128))

    sums_in = gathered.at[pl.ds(0, count - 1)]
    pltpu.make_async_copy(sums_in, sums_in, sum_recv).wait()
    total = jnp.sum(gathered[...], axis=0)
    coeffs = [solve(total, field, used_ref) for field in range(2)]

    piece = ne // PIECES
    groups = piece // 8

    def mix(which, start_group, stop_group):
        def body(group, carry):
            first = pl.multiple_of(group * 8, 8)
            for row in which:
                source = pl.ds(first * rows + row, 8, stride=rows)
                for field in range(2):
                    value = coeffs[field][0] * base[field, source, :]
                    for index in range(HISTORY):
                        value = value + coeffs[field][index + 1] * hist[index, field, source, :]
                    mixed[row, field, pl.ds(first, 8), :] = value
            return carry

        lax.fori_loop(start_group, stop_group, body, 0)

    sends = []
    for index in range(PIECES):
        mix((0, rows - 1), index * groups, (index + 1) * groups)
        span = pl.ds(index * piece, piece)
        up = pltpu.make_async_remote_copy(
            mixed.at[rows - 1, :, span], lo.at[:, span], edge_send.at[0, index],
            edge_recv.at[0, index], device_id=(my_e, next_s), device_id_type=MESH,
        )
        down = pltpu.make_async_remote_copy(
            mixed.at[0, :, span], hi.at[:, span], edge_send.at[1, index],
            edge_recv.at[1, index], device_id=(my_e, prev_s), device_id_type=MESH,
        )
        sends.append((up, down))

        @pl.when(has_above)
        def _():
            up.start()

        @pl.when(has_below)
        def _():
            down.start()

    def drift(which, start_group, stop_group):
        def body(group, carry):
            first = pl.multiple_of(group * 8, 8)
            span = pl.ds(first, 8)
            energy = my_e * ne + first + lax.broadcasted_iota(jnp.int32, (8, 128), 0)
            drive = 0.25 * dos_of(energy)
            for row in which:
                own = [mixed[row, field, span, :] for field in range(2)]
                for field in range(2):
                    value = own[field]
                    under = lo[field, span, :] if row == 0 else mixed[row - 1, field, span, :]
                    over = (
                        hi[field, span, :] if row == rows - 1 else mixed[row + 1, field, span, :]
                    )
                    result = (
                        weight[row, 0] * value
                        + weight[row, 1] * under
                        + weight[row, 2] * over
                        + weight[row, 3] * pltpu.roll(value, 1, 1)
                        + weight[row, 4] * pltpu.roll(value, 127, 1)
                        + weight[row, 5] * pltpu.roll(value, COLS, 1)
                    )
                    if field == 0:
                        result = result + drive * own[1]
                    else:
                        result = result - drive * own[0]
                    out[field, pl.ds(first * rows + row, 8, stride=rows), :] = result
            return carry

        lax.fori_loop(start_group, stop_group, body, 0)

    inner = tuple(range(1, rows - 1))
    if inner:
        mix(inner, 0, PIECES * groups)
        drift(inner, 0, PIECES * groups)

    stores = []
    for index in range(PIECES):
        up, down = sends[index]

        @pl.when(has_below)
        def _():
            up.wait_recv()

        @pl.when(has_above)
        def _():
            down.wait_recv()

        drift((0, rows - 1), index * groups, (index + 1) * groups)
        span = pl.ds(index * piece * rows, piece * rows)
        store = pltpu.make_async_copy(out.at[:, span], out_hbm.at[:, span], out_sem.at[index])
        store.start()
        stores.append(store)

    sums_out = gathered.at[pl.ds(0, count - 1)]
    pltpu.make_async_copy(sums_out, sums_out, sum_send).wait()

    @pl.when(has_above_e)
    def _():
        up_e.wait_send()

    @pl.when(has_below_e)
    def _():
        down_e.wait_send()

    @pl.when(has_above)
    def _():
        up_mob.wait_send()
        for up, _ in sends:
            up.wait_send()

    @pl.when(has_below)
    def _():
        down_mob.wait_send()
        for _, down in sends:
            down.wait_send()

    for store in stores:
        store.wait()


def local(n_egrp, n_space, dist, hist_x, hist_g, mobility, region, phonon_bins, coupling, hist_used):
    ne, rows = dist.shape[1], dist.shape[2]
    total = ne * rows
    pad = KMAX * rows
    count = n_egrp * n_space
    f32 = jnp.float32
    smem = pl.BlockSpec(memory_space=pltpu.SMEM)
    vmem = pl.BlockSpec(memory_space=pltpu.VMEM)
    hbm = pl.BlockSpec(memory_space=pl.ANY)
    result = pl.pallas_call(
        functools.partial(kernel, n_egrp, n_space, ne, rows),
        out_shape=jax.ShapeDtypeStruct((2, total, 128), f32),
        in_specs=[smem, smem, smem, vmem, vmem, hbm, hbm, hbm],
        out_specs=hbm,
        scratch_shapes=[
            pltpu.VMEM((total + 2 * pad, 128), f32),
            pltpu.VMEM((total, 128), f32),
            pltpu.VMEM((HISTORY, 2, total, 128), jnp.bfloat16),
            pltpu.VMEM((HISTORY, 2, total, 128), jnp.bfloat16),
            pltpu.VMEM((2, total, 128), f32),
            pltpu.VMEM((HISTORY, 2, total, 128), f32),
            pltpu.VMEM((rows, 2, ne, 128), f32),
            pltpu.VMEM((2, total, 128), f32),
            pltpu.VMEM((2, ne, 128), f32),
            pltpu.VMEM((2, ne, 128), f32),
            pltpu.VMEM((STEP, 128), jnp.int32),
            pltpu.VMEM((STEP, 128), f32),
            pltpu.VMEM((STEP, 128), jnp.int32),
            pltpu.VMEM((rows, 6, 8, 128), f32),
            pltpu.VMEM((2, 1, 128), f32),
            pltpu.VMEM((1, 128), f32),
            pltpu.VMEM((1, 128), f32),
            pltpu.VMEM((32, 128), f32),
            pltpu.VMEM((1, 128), f32),
            pltpu.VMEM((count, 1, 128), f32),
            pltpu.VMEM((2, pad, 128), f32),
            pltpu.SemaphoreType.DMA((2 + 2 * HISTORY,)),
            pltpu.SemaphoreType.DMA((PIECES,)),
            pltpu.SemaphoreType.DMA((2,)),
            pltpu.SemaphoreType.DMA((2,)),
            pltpu.SemaphoreType.DMA((2,)),
            pltpu.SemaphoreType.DMA((2,)),
            pltpu.SemaphoreType.DMA,
            pltpu.SemaphoreType.DMA,
            pltpu.SemaphoreType.DMA((2, PIECES)),
            pltpu.SemaphoreType.DMA((2, PIECES)),
        ],
        compiler_params=pltpu.CompilerParams(
            collective_id=0, has_side_effects=True, vmem_limit_bytes=48 << 20
        ),
    )(
        phonon_bins, coupling, hist_used, mobility, region,
        dist.reshape(2, total, 128),
        hist_x.reshape(HISTORY, 2, total, 128),
        hist_g.reshape(HISTORY, 2, total, 128),
    )
    return result.reshape(dist.shape)


def solution(mesh):
    in_specs = (
        P(None, "egrp", "space", None),
        P(None, None, "egrp", "space", None),
        P(None, None, "egrp", "space", None),
        P("space", None),
        P("space", None),
        P(),
        P(),
        P(),
    )
    out_specs = P(None, "egrp", "space", None)
    body = functools.partial(local, mesh.shape["egrp"], mesh.shape["space"])
    return jax.shard_map(body, mesh=mesh, in_specs=in_specs, out_specs=out_specs, check_vma=False)
```

time: 197 us -> 38.6 us (0.20)
  local copies, waits for them, and re-layouts: 57.4 us -> 6.26 us
  other arithmetic: 45.2 us -> 0 us
  blocking collectives: 42.1 us -> 0 us
  Pallas kernels: 0 us -> 32.1 us
  starting transfers between devices: 18.5 us -> 0 us
  matrix products: 11.5 us -> 0 us
  between operations: 10.7 us -> 0.02 us
  waiting for transfers between devices: 9.76 us -> 0 us
    psum x1 -> x0, blocking collectives: 42.1 us -> none  [local(): lax.psum((among, cross, self_term), ('egrp', 'space'))]
    pallas_call x0 -> x1, Pallas kernels: none -> 32.1 us  [local(): pl.pallas_call(functools.partial(kernel, n_egrp, n_space, ne, rows), out_...]
    unnamed x66 -> x13, local copies, waits for them, and re-layouts: 29.2 us -> 6.26 us
    add x6 -> x0, other arithmetic: 15.4 us -> none  [the longest x2 11.7 us: local(): part_mix + coeffs[index + 1] * (hist_x[index, field].astype(jnp.float32)...]
    slice x10 -> x0, local copies, waits for them, and re-layouts: 13.3 us -> none  [the longest x1 4.14 us: local(): hist_x[index, field].astype(jnp.float32)]
    ppermute x4 -> x0, starting transfers between devices: 11.1 us -> none  [the longest x2 7.28 us: extended(): lax.ppermute(lax.slice_in_dim(block, 0, width, axis=dim), axis, backward)]
    ppermute x4 -> x0, waiting for transfers between devices: 9.76 us -> none  [the longest x2 9.75 us: extended(): lax.ppermute(lax.slice_in_dim(block, block.shape[dim] - width, None, axis...]
    dot_general x1 -> x0, matrix products: 9.54 us -> none  [local(): lax.dot_general(flat_g, flat_g, (((2,), (2,)), ((1,), (1,))), preferred_e...]
  transfers between devices with their start and end apart: 6 -> 0, of which waited for: 1 -> 0; matrix products, arithmetic and copies ran while one was open for 32% -> 0% of each run, Pallas kernels for 0% -> 0%
where the time goes in v1:
time: 38.6 us; the launch traced here: 38.4 us
  Pallas kernels  32.1 us (83%)
  local copies, waits for them, and re-layouts  6.26 us (16%)
    pallas_call x1, Pallas kernels, local(): pl.pallas_call(functools.partial(kernel, n_egrp, n_space, ne, rows), out_...  32.1 us
    unnamed x13, local copies, waits for them, and re-layouts  6.26 us

profile of v1, /device:TPU:4, one launch (start us, length us, event | category | flops | bytes accessed | tf_op | source)
XLA Modules:
  0.0 38.4 jit_solution(5049980626372699088)
XLA Ops:
  0.0 0.0 copy-start
  0.0 1.6 %copy-done = f32[2,512,4,128]{3,2,1,0:T(4,128)S(1)} copy-done((f32[2,512,4,128]{3,2,1,0:T(4,128)S(1)}, f32[2,512,4,128]{3,2,1,0:T(4,128)}, u32[]{:S(2)}) %copy-start) | copy-done | bytes 2097176
  1.6 0.0 copy-start.1
  1.6 0.7 %copy-done.1 = f32[4,128]{1,0:T(4,128)S(1)} copy-done((f32[4,128]{1,0:T(4,128)S(1)}, f32[4,128]{1,0:T(4,128)}, u32[]{:S(2)}) %copy-start.1) | copy-done | bytes 2072
  2.3 0.0 copy-start.2
  2.3 0.7 %copy-done.2 = s32[4,128]{1,0:T(4,128)S(1)} copy-done((s32[4,128]{1,0:T(4,128)S(1)}, s32[4,128]{1,0:T(4,128)}, u32[]{:S(2)}) %copy-start.2) | copy-done | bytes 2072
  3.0 0.0 copy-start.3
  3.0 0.7 %copy-done.3 = s32[2,4]{1,0:T(2,128)S(1)} copy-done((s32[2,4]{1,0:T(2,128)S(1)}, s32[2,4]{1,0:T(2,128)}, u32[]{:S(2)}) %copy-start.3) | copy-done | bytes 56
  3.6 0.0 copy-start.4
  3.6 0.7 %copy-done.4 = s32[4]{0:T(128)S(1)} copy-done((s32[4]{0:T(128)S(1)}, s32[4]{0:T(128)}, u32[]{:S(2)}) %copy-start.4) | copy-done | bytes 40
  4.3 0.0 copy-start.5
  4.3 0.7 %copy-done.5 = f32[4]{0:T(128)S(1)} copy-done((f32[4]{0:T(128)S(1)}, f32[4]{0:T(128)}, u32[]{:S(2)}) %copy-start.5) | copy-done | bytes 40
  4.9 32.1 %shard_map.82 = f32[2,2048,128]{2,1,0:T(8,128)S(1)} custom-call(s32[4]{0:T(128)S(1)} %copy-done.4, f32[4]{0:T(128)S(1)} %copy-done.5, s32[2,4]{1,0:T(2,128)S(1)} %copy-done.3, f32[4,128]{1,0:T(4,128)S(1)} %copy-done.1, s32[4,128]{1,0:T(4,128)S(1)} %copy-done.2, f32[2,2048,128]{2,1,0:T(8,128)S(1)} %bitcast.5, bf16[4,2,2048,128]{3,2,1,0:T(8,128)(2,1)} %bitcast.6, ...), custom_call_target="tpu_custom_call" | custom-call | tf_op jit(solution)/shard_map/pallas_call | solution.py:437
  37.0 1.3 %copy.10 = f32[2,512,4,128]{3,2,1,0:T(4,128)} copy(f32[2,512,4,128]{3,2,1,0:T(4,128)S(1)} %bitcast.4) | data formatting | bytes 4194304
Async XLA Ops:
  0.0 1.6 %copy-start = (f32[2,512,4,128]{3,2,1,0:T(4,128)S(1)}, f32[2,512,4,128]{3,2,1,0:T(4,128)}, u32[]{:S(2)}) copy-start(f32[2,512,4,128]{3,2,1,0:T(4,128)} %param.8) | copy-start | bytes 6291460
  1.6 0.7 %copy-start.1 = (f32[4,128]{1,0:T(4,128)S(1)}, f32[4,128]{1,0:T(4,128)}, u32[]{:S(2)}) copy-start(f32[4,128]{1,0:T(4,128)} %mob_ref.1) | copy-start | bytes 6148
  2.3 0.7 %copy-start.2 = (s32[4,128]{1,0:T(4,128)S(1)}, s32[4,128]{1,0:T(4,128)}, u32[]{:S(2)}) copy-start(s32[4,128]{1,0:T(4,128)} %region_ref.1) | copy-start | bytes 6148
  3.0 0.7 %copy-start.3 = (s32[2,4]{1,0:T(2,128)S(1)}, s32[2,4]{1,0:T(2,128)}, u32[]{:S(2)}) copy-start(s32[2,4]{1,0:T(2,128)} %used_ref.1) | copy-start | bytes 100
  3.6 0.7 %copy-start.4 = (s32[4]{0:T(128)S(1)}, s32[4]{0:T(128)}, u32[]{:S(2)}) copy-start(s32[4]{0:T(128)} %bins_ref.1) | copy-start | bytes 52
  4.3 0.7 %copy-start.5 = (f32[4]{0:T(128)S(1)}, f32[4]{0:T(128)}, u32[]{:S(2)}) copy-start(f32[4]{0:T(128)} %coup_ref.1) | copy-start | bytes 52

commit v2 on v1

--- a/solution.py
+++ b/solution.py
@@ -13,6 +13,7 @@
 COLS = 64
 PIECES = 4
 STEP = 16
+WIDE = 32
 PAIRS = [(i, j) for i in range(HISTORY + 1) for j in range(i, HISTORY + 1)]
 MESH = pl.DeviceIdType.MESH
 
@@ -63,11 +64,12 @@
 
 def kernel(
     n_egrp, n_space, ne, rows,
-    bins_ref, coup_ref, used_ref, mob_ref, region_ref, dist_hbm, hx_hbm, hg_hbm,
-    out_hbm,
-    even, odd, hg, hx, base, hist, mixed, out, lo, hi, offs, lam_ref, tile, weight,
+    bins_hbm, coup_hbm, used_hbm, mob_hbm, region_hbm, dist_hbm, hx_hbm, hg_hbm,
+    out,
+    bins_ref, coup_ref, used_ref, mob_ref, region_ref,
+    even, odd, hg, hx, base, hist, mixed, packed, lo, hi, offs, lam_ref, tile, weight,
     mob_send, mob_lo, mob_hi, sums, part, gathered, halo,
-    in_sem, out_sem, halo_send, halo_recv, mob_ssem, mob_rsem, sum_send, sum_recv,
+    in_sem, small_sem, halo_send, halo_recv, mob_ssem, mob_rsem, sum_send, sum_recv,
     edge_send, edge_recv,
 ):
     my_e = lax.axis_index("egrp")
@@ -80,6 +82,13 @@
     def device(index):
         return (index // n_space, lax.rem(index, n_space))
 
+    small = [
+        pltpu.make_async_copy(source, target, small_sem.at[index])
+        for index, (source, target) in enumerate((
+            (region_hbm, region_ref), (bins_hbm, bins_ref), (coup_hbm, coup_ref),
+            (mob_hbm, mob_ref), (used_hbm, used_ref),
+        ))
+    ]
     loads = [
         pltpu.make_async_copy(dist_hbm.at[0], even.at[pl.ds(pad, total_rows)], in_sem.at[0]),
         pltpu.make_async_copy(dist_hbm.at[1], odd, in_sem.at[1]),
@@ -90,7 +99,7 @@
         pltpu.make_async_copy(hx_hbm.at[index], hx.at[index], in_sem.at[2 + HISTORY + index])
         for index in range(HISTORY)
     ]
-    for copy in loads + late:
+    for copy in small + loads + late:
         copy.start()
 
     barrier = pltpu.get_barrier_semaphore()
@@ -103,6 +112,8 @@
 
     lax.fori_loop(1, count, greet, 0)
 
+    for copy in small:
+        copy.wait()
     for copy_of in range(STEP // rows):
         tile[pl.ds(copy_of * rows, rows), :] = region_ref[...]
     region = tile[...]
@@ -122,6 +133,9 @@
     has_below = my_s > 0
     has_above = my_s < n_space - 1
 
+    for field in range(2):
+        mixed[field, pl.ds(0, 8), :] = jnp.zeros((8, 128), jnp.float32)
+        mixed[field, pl.ds(8 + total_rows, 8), :] = jnp.zeros((8, 128), jnp.float32)
     even[pl.ds(0, pad), :] = jnp.zeros((pad, 128), jnp.float32)
     even[pl.ds(pad + total_rows, pad), :] = jnp.zeros((pad, 128), jnp.float32)
 
@@ -283,6 +297,7 @@
 
     lanes = lax.broadcasted_iota(jnp.int32, (1, 128), 1)
     column = lanes % COLS
+    none = jnp.zeros((1, 128), jnp.float32)
     for row in range(rows):
         mob = mob_ref[row : row + 1, :]
         under = mob_lo[...] if row == 0 else mob_ref[row - 1 : row, :]
@@ -297,41 +312,59 @@
         w_right = jnp.where(column < COLS - 1, 0.04 * (mob + pltpu.roll(mob, 127, 1)), 0.0)
         w_plane = 0.04 * (mob + pltpu.roll(mob, COLS, 1))
         own = 1.0 - (w_under + w_over + w_left + w_right + w_plane)
-        for place, value in enumerate((own, w_under, w_over, w_left, w_right, w_plane)):
-            weight[row, place] = jnp.broadcast_to(value, (8, 128))
+        parts = (
+            own,
+            none if row == 0 else w_under,
+            none if row == rows - 1 else w_over,
+            w_left,
+            w_right,
+            w_plane,
+            w_under if row == 0 else w_over if row == rows - 1 else none,
+        )
+        for place, value in enumerate(parts):
+            for copy_of in range(8 // rows):
+                weight[place, copy_of * rows + row : copy_of * rows + row + 1, :] = value
 
     sums_in = gathered.at[pl.ds(0, count - 1)]
     pltpu.make_async_copy(sums_in, sums_in, sum_recv).wait()
     total = jnp.sum(gathered[...], axis=0)
-    coeffs = [solve(total, field, used_ref) for field in range(2)]
+    coeffs = [
+        [jnp.concatenate([c] * (WIDE // 8), axis=0) for c in solve(total, field, used_ref)]
+        for field in range(2)
+    ]
 
     piece = ne // PIECES
-    groups = piece // 8
-
-    def mix(which, start_group, stop_group):
-        def body(group, carry):
-            first = pl.multiple_of(group * 8, 8)
-            for row in which:
-                source = pl.ds(first * rows + row, 8, stride=rows)
-                for field in range(2):
-                    value = coeffs[field][0] * base[field, source, :]
-                    for index in range(HISTORY):
-                        value = value + coeffs[field][index + 1] * hist[index, field, source, :]
-                    mixed[row, field, pl.ds(first, 8), :] = value
-            return carry
-
-        lax.fori_loop(start_group, stop_group, body, 0)
+    blocks = piece * rows // WIDE
+
+    def mix(block, carry):
+        row = pl.multiple_of(block * WIDE, WIDE)
+        for field in range(2):
+            value = coeffs[field][0] * base[field, pl.ds(row, WIDE), :]
+            for index in range(HISTORY):
+                value = value + coeffs[field][index + 1] * hist[index, field, pl.ds(row, WIDE), :]
+            mixed[field, pl.ds(8 + row, WIDE), :] = value
+        return carry
+
+    def pack(group, carry):
+        first = pl.multiple_of(group * 8, 8)
+        for field in range(2):
+            for side, row in ((0, 0), (1, rows - 1)):
+                packed[side, field, pl.ds(first, 8), :] = mixed[
+                    field, pl.ds(8 + first * rows + row, 8, stride=rows), :
+                ]
+        return carry
 
     sends = []
     for index in range(PIECES):
-        mix((0, rows - 1), index * groups, (index + 1) * groups)
+        lax.fori_loop(index * blocks, (index + 1) * blocks, mix, 0)
+        lax.fori_loop(index * (piece // 8), (index + 1) * (piece // 8), pack, 0)
         span = pl.ds(index * piece, piece)
         up = pltpu.make_async_remote_copy(
-            mixed.at[rows - 1, :, span], lo.at[:, span], edge_send.at[0, index],
+            packed.at[1, :, span], lo.at[:, span], edge_send.at[0, index],
             edge_recv.at[0, index], device_id=(my_e, next_s), device_id_type=MESH,
         )
         down = pltpu.make_async_remote_copy(
-            mixed.at[0, :, span], hi.at[:, span], edge_send.at[1, index],
+            packed.at[0, :, span], hi.at[:, span], edge_send.at[1, index],
             edge_recv.at[1, index], device_id=(my_e, prev_s), device_id_type=MESH,
         )
         sends.append((up, down))
@@ -344,43 +377,56 @@
         def _():
             down.start()
 
-    def drift(which, start_group, stop_group):
-        def body(group, carry):
-            first = pl.multiple_of(group * 8, 8)
-            span = pl.ds(first, 8)
-            energy = my_e * ne + first + lax.broadcasted_iota(jnp.int32, (8, 128), 0)
+    weights = [weight[place] for place in range(7)]
+
+    def drift(block, carry):
+        for part_of in range(WIDE // 8):
+            row = pl.multiple_of(block * WIDE + part_of * 8, 8)
+            energy = my_e * ne + (row + lax.broadcasted_iota(jnp.int32, (8, 128), 0)) // rows
             drive = 0.25 * dos_of(energy)
-            for row in which:
-                own = [mixed[row, field, span, :] for field in range(2)]
-                for field in range(2):
-                    value = own[field]
-                    under = lo[field, span, :] if row == 0 else mixed[row - 1, field, span, :]
-                    over = (
-                        hi[field, span, :] if row == rows - 1 else mixed[row + 1, field, span, :]
-                    )
-                    result = (
-                        weight[row, 0] * value
-                        + weight[row, 1] * under
-                        + weight[row, 2] * over
-                        + weight[row, 3] * pltpu.roll(value, 1, 1)
-                        + weight[row, 4] * pltpu.roll(value, 127, 1)
-                        + weight[row, 5] * pltpu.roll(value, COLS, 1)
-                    )
-                    if field == 0:
-                        result = result + drive * own[1]
+            own = [mixed[field, pl.ds(8 + row, 8), :] for field in range(2)]
+            for field in range(2):
+                value = own[field]
+                result = (
+                    weights[0] * value
+                    + weights[1] * mixed[field, pl.ds(7 + row, 8), :]
+                    + weights[2] * mixed[field, pl.ds(9 + row, 8), :]
+                    + weights[3] * pltpu.roll(value, 1, 1)
+                    + weights[4] * pltpu.roll(value, 127, 1)
+                    + weights[5] * pltpu.roll(value, COLS, 1)
+                )
+                if field == 0:
+                    result = result + drive * own[1]
+                else:
+                    result = result - drive * own[0]
+                out[field, pl.ds(row, 8), :] = result
+        return carry
+
+    lax.fori_loop(0, PIECES * blocks, drift, 0)
+
+    sublane = lax.broadcasted_iota(jnp.int32, (8, 128), 0)
+    places = [
+        (sublane < (copy_of * rows + rows // 2), sublane < (copy_of + 1) * rows)
+        for copy_of in range(8 // rows)
+    ]
+
+    def add_edges(block, carry):
+        for part_of in range(WIDE // 8):
+            row = pl.multiple_of(block * WIDE + part_of * 8, 8)
+            first = block * (WIDE // rows) + part_of * (8 // rows)
+            for field in range(2):
+                value = None
+                for copy_of in reversed(range(8 // rows)):
+                    from_hi = hi[field, pl.ds(first + copy_of, 8, stride=0), :]
+                    from_lo = lo[field, pl.ds(first + copy_of, 8, stride=0), :]
+                    if value is None:
+                        value = from_hi
                     else:
-                        result = result - drive * own[0]
-                    out[field, pl.ds(first * rows + row, 8, stride=rows), :] = result
-            return carry
-
-        lax.fori_loop(start_group, stop_group, body, 0)
-
-    inner = tuple(range(1, rows - 1))
-    if inner:
-        mix(inner, 0, PIECES * groups)
-        drift(inner, 0, PIECES * groups)
-
-    stores = []
+                        value = jnp.where(places[copy_of][1], from_hi, value)
+                    value = jnp.where(places[copy_of][0], from_lo, value)
+                out[field, pl.ds(row, 8), :] = out[field, pl.ds(row, 8), :] + weights[6] * value
+        return carry
+
     for index in range(PIECES):
         up, down = sends[index]
 
@@ -392,11 +438,7 @@
         def _():
             down.wait_recv()
 
-        drift((0, rows - 1), index * groups, (index + 1) * groups)
-        span = pl.ds(index * piece * rows, piece * rows)
-        store = pltpu.make_async_copy(out.at[:, span], out_hbm.at[:, span], out_sem.at[index])
-        store.start()
-        stores.append(store)
+        lax.fori_loop(index * blocks, (index + 1) * blocks, add_edges, 0)
 
     sums_out = gathered.at[pl.ds(0, count - 1)]
     pltpu.make_async_copy(sums_out, sums_out, sum_send).wait()
@@ -420,9 +462,6 @@
         down_mob.wait_send()
         for _, down in sends:
             down.wait_send()
-
-    for store in stores:
-        store.wait()
 
 
 def local(n_egrp, n_space, dist, hist_x, hist_g, mobility, region, phonon_bins, coupling, hist_used):
@@ -431,29 +470,33 @@
     pad = KMAX * rows
     count = n_egrp * n_space
     f32 = jnp.float32
-    smem = pl.BlockSpec(memory_space=pltpu.SMEM)
     vmem = pl.BlockSpec(memory_space=pltpu.VMEM)
-    hbm = pl.BlockSpec(memory_space=pl.ANY)
+    hbm = pl.BlockSpec(memory_space=pltpu.HBM)
     result = pl.pallas_call(
         functools.partial(kernel, n_egrp, n_space, ne, rows),
         out_shape=jax.ShapeDtypeStruct((2, total, 128), f32),
-        in_specs=[smem, smem, smem, vmem, vmem, hbm, hbm, hbm],
-        out_specs=hbm,
+        in_specs=[hbm] * 8,
+        out_specs=vmem,
         scratch_shapes=[
+            pltpu.SMEM((NREGION,), jnp.int32),
+            pltpu.SMEM((NREGION,), f32),
+            pltpu.SMEM((2, HISTORY), jnp.int32),
+            pltpu.VMEM((rows, 128), f32),
+            pltpu.VMEM((rows, 128), jnp.int32),
             pltpu.VMEM((total + 2 * pad, 128), f32),
             pltpu.VMEM((total, 128), f32),
             pltpu.VMEM((HISTORY, 2, total, 128), jnp.bfloat16),
             pltpu.VMEM((HISTORY, 2, total, 128), jnp.bfloat16),
             pltpu.VMEM((2, total, 128), f32),
             pltpu.VMEM((HISTORY, 2, total, 128), f32),
-            pltpu.VMEM((rows, 2, ne, 128), f32),
-            pltpu.VMEM((2, total, 128), f32),
+            pltpu.VMEM((2, total + 16, 128), f32),
+            pltpu.VMEM((2, 2, ne, 128), f32),
             pltpu.VMEM((2, ne, 128), f32),
             pltpu.VMEM((2, ne, 128), f32),
             pltpu.VMEM((STEP, 128), jnp.int32),
             pltpu.VMEM((STEP, 128), f32),
             pltpu.VMEM((STEP, 128), jnp.int32),
-            pltpu.VMEM((rows, 6, 8, 128), f32),
+            pltpu.VMEM((7, 8, 128), f32),
             pltpu.VMEM((2, 1, 128), f32),
             pltpu.VMEM((1, 128), f32),
             pltpu.VMEM((1, 128), f32),
@@ -462,7 +505,7 @@
             pltpu.VMEM((count, 1, 128), f32),
             pltpu.VMEM((2, pad, 128), f32),
             pltpu.SemaphoreType.DMA((2 + 2 * HISTORY,)),
-            pltpu.SemaphoreType.DMA((PIECES,)),
+            pltpu.SemaphoreType.DMA((5,)),
             pltpu.SemaphoreType.DMA((2,)),
             pltpu.SemaphoreType.DMA((2,)),
             pltpu.SemaphoreType.DMA((2,)),
@@ -473,13 +516,13 @@
             pltpu.SemaphoreType.DMA((2, PIECES)),
         ],
         compiler_params=pltpu.CompilerParams(
-            collective_id=0, has_side_effects=True, vmem_limit_bytes=48 << 20
+            collective_id=0, has_side_effects=True, vmem_limit_bytes=40 << 20
         ),
     )(
-        phonon_bins, coupling, hist_used, mobility, region,
+        *[pltpu.with_memory_space_constraint(x, pltpu.HBM) for x in (phonon_bins, coupling, hist_used, mobility, region,
         dist.reshape(2, total, 128),
         hist_x.reshape(HISTORY, 2, total, 128),
-        hist_g.reshape(HISTORY, 2, total, 128),
+        hist_g.reshape(HISTORY, 2, total, 128))],
     )
     return result.reshape(dist.shape)
 

time: 38.6 us -> 32.9 us (0.85)
  local copies, waits for them, and re-layouts: 6.26 us -> 1.32 us
  Pallas kernels: 32.1 us -> 31.5 us
    unnamed x13 -> x1, local copies, waits for them, and re-layouts: 6.26 us -> 1.32 us
    pallas_call x1, Pallas kernels: 32.1 us -> 31.5 us  [local(): pl.pallas_call(functools.partial(kernel, n_egrp, n_space, ne, rows), out_...]
where the time goes in v2:
time: 32.9 us; the launch traced here: 32.8 us
  Pallas kernels  31.5 us (96%)
  local copies, waits for them, and re-layouts  1.32 us (4%)
    pallas_call x1, Pallas kernels, local(): pl.pallas_call(functools.partial(kernel, n_egrp, n_space, ne, rows), out_...  31.5 us
    unnamed x1, local copies, waits for them, and re-layouts  1.32 us

profile of v2, /device:TPU:4, one launch (start us, length us, event | category | flops | bytes accessed | tf_op | source)
XLA Modules:
  0.0 32.8 jit_solution(9301273522250958711)
XLA Ops:
  0.0 31.5 %shard_map.82 = f32[2,2048,128]{2,1,0:T(8,128)S(1)} custom-call(s32[4]{0:T(128)} %bins_hbm.1, f32[4]{0:T(128)} %coup_hbm.1, s32[2,4]{1,0:T(2,128)} %used_hbm.1, f32[4,128]{1,0:T(4,128)} %mob_hbm.1, s32[4,128]{1,0:T(4,128)} %region_hbm.1, f32[2,2048,128]{2,1,0:T(8,128)} %bitcast.7, bf16[4,2,2048,128]{3,2,1,0:T(8,128)(2,1)} %bitcast.5, ...), custom_call_target="tpu_custom_call" | custom-call | tf_op jit(solution)/shard_map/pallas_call | solution.py:475
  31.5 1.3 %copy.10 = f32[2,512,4,128]{3,2,1,0:T(4,128)} copy(f32[2,512,4,128]{3,2,1,0:T(4,128)S(1)} %bitcast.4) | data formatting | bytes 4194304

commit v3 on v2

--- a/solution.py
+++ b/solution.py
@@ -12,14 +12,15 @@
 KMAX = 64
 COLS = 64
 PIECES = 4
-STEP = 16
+STEP = 32
 WIDE = 32
 PAIRS = [(i, j) for i in range(HISTORY + 1) for j in range(i, HISTORY + 1)]
 MESH = pl.DeviceIdType.MESH
 
 
 def dos_of(energy):
-    return jnp.sqrt((energy.astype(jnp.float32) + 0.5) * (1.0 / NE))
+    value = (energy.astype(jnp.float32) + 0.5) * (1.0 / NE)
+    return value * lax.rsqrt(value)
 
 
 def solve(total, field, used_ref):
@@ -214,10 +215,11 @@
         loss = 1.0 + lam * (1.5 * dos_low + 0.5 * dos_high)
         own_even = even[pl.ds(pad + row, STEP), :]
         own_odd = odd[pl.ds(row, STEP), :]
+        both = 1.0 / (loss * (loss + lam))
         gain = lam * dos_of(energy) * (1.5 * above + 0.5 * below)
         res = [
-            (own_even + gain) * (1.0 / loss) - own_even,
-            own_odd * (1.0 / (loss + lam)) - own_odd,
+            (own_even + gain) * (both * (loss + lam)) - own_even,
+            own_odd * (both * loss) - own_odd,
         ]
         base[0, pl.ds(row, STEP), :] = own_even + 0.5 * res[0]
         base[1, pl.ds(row, STEP), :] = own_odd + 0.5 * res[1]
@@ -229,7 +231,7 @@
             ]
             for position, (i, j) in enumerate(PAIRS):
                 product = vectors[i] * vectors[j]
-                new.append(accs[field * len(PAIRS) + position] + (product[:8] + product[8:]))
+                new.append(accs[field * len(PAIRS) + position] + jnp.sum(product.reshape(STEP // 8, 8, 128), axis=0))
         return tuple(new)
 
     accs = tuple(jnp.zeros((8, 128), jnp.float32) for _ in range(2 * len(PAIRS)))

time: 32.9 us -> 31.5 us (0.957)
  Pallas kernels: 31.5 us -> 30.1 us
    pallas_call x1, Pallas kernels: 31.5 us -> 30.1 us  [local(): pl.pallas_call(functools.partial(kernel, n_egrp, n_space, ne, rows), out_...]
where the time goes in v3:
time: 31.5 us; the launch traced here: 31.4 us
  Pallas kernels  30.1 us (96%)
  local copies, waits for them, and re-layouts  1.32 us (4%)
    pallas_call x1, Pallas kernels, local(): pl.pallas_call(functools.partial(kernel, n_egrp, n_space, ne, rows), out_...  30.1 us
    unnamed x1, local copies, waits for them, and re-layouts  1.32 us

profile of v3, /device:TPU:4, one launch (start us, length us, event | category | flops | bytes accessed | tf_op | source)
XLA Modules:
  0.0 31.4 jit_solution(6554672763626236182)
XLA Ops:
  0.0 30.1 %shard_map.82 = f32[2,2048,128]{2,1,0:T(8,128)S(1)} custom-call(s32[4]{0:T(128)} %bins_hbm.1, f32[4]{0:T(128)} %coup_hbm.1, s32[2,4]{1,0:T(2,128)} %used_hbm.1, f32[4,128]{1,0:T(4,128)} %mob_hbm.1, s32[4,128]{1,0:T(4,128)} %region_hbm.1, f32[2,2048,128]{2,1,0:T(8,128)} %bitcast.7, bf16[4,2,2048,128]{3,2,1,0:T(8,128)(2,1)} %bitcast.5, ...), custom_call_target="tpu_custom_call" | custom-call | tf_op jit(solution)/shard_map/pallas_call | solution.py:477
  30.1 1.3 %copy.10 = f32[2,512,4,128]{3,2,1,0:T(4,128)} copy(f32[2,512,4,128]{3,2,1,0:T(4,128)S(1)} %bitcast.4) | data formatting | bytes 4194304
